TPU v7x, 256 devices: a whole 4x4x8 slice. The times are simulated.
256 devices in a mesh: ctx: 32 (over x, y, core), head: 8 (over z).
Axes of the slice: x: 4, y: 4, z: 8, core: 2. Of those that a mesh axis runs over, the one named last changes fastest.
Arguments:
- queries: bfloat16 [2, 6144, 4096], P(None, 'ctx', 'head'), may hold values from -6 to 6
- key_rows: bfloat16 [2, 6144, 4096], P(None, 'ctx', 'head'), may hold values from -6 to 6
- value_rows: bfloat16 [2, 6144, 4096], P(None, 'ctx', 'head'), may hold values from -6 to 6
- out_weight: bfloat16 [4096, 4096], P('head'), may hold values from -0.09375 to 0.09375
- cotangent: bfloat16 [2, 6144, 4096], P(None, 'ctx', 'head'), may hold values from -6 to 6
Outputs:
- layer_output: bfloat16 [2, 6144, 4096], P(None, 'ctx', 'head')
- query_grad: bfloat16 [2, 6144, 4096], P(None, 'ctx', 'head')
- key_grad: bfloat16 [2, 6144, 4096], P(None, 'ctx', 'head')
- value_grad: bfloat16 [2, 6144, 4096], P(None, 'ctx', 'head')
- weight_grad: float32 [4096, 4096], P('head', 'ctx')
All inputs are finite; a program needn't handle non-finite values.
Results may differ from a plain program's by a relative error of at most 0.015.
Values may be sent and summed in bfloat16 or wider, within the bound.
No kernel may reach another device: no remote copies, remote signals or barrier semaphores. Data moves between devices by JAX's collectives and lax.ppermute only.
A program may use at most 128 MiB of HBM per device.

v0:
```python
import jax
import jax.numpy as jnp
from jax import lax
from jax.sharding import Mesh
from jax.sharding import PartitionSpec as P

DH = 128
CTX = ("ctx_0", "ctx_1", "ctx_2")
epsilon = 1e-06


def filled_with(value, identity):
    return jnp.broadcast_to(jnp.asarray(identity, value.dtype), value.shape)


def prefix_by_axis(value, axes, combine, identity, reverse):
    before = start = filled_with(value, identity)
    subtotal = value
    for axis in reversed(axes):
        count, index = (lax.axis_size(axis), lax.axis_index(axis))
        pieces = lax.all_gather(subtotal, axis)
        inside, subtotal = (start, start)
        for k in reversed(range(count)) if reverse else range(count):
            passed = k > index if reverse else k < index
            subtotal = combine(subtotal, pieces[k])
            inside = jnp.where(passed, subtotal, inside)
        before = combine(inside, before)
    return before


def in_blocks(value, dim, count):
    before, after = (value.shape[:dim], value.shape[dim + 1 :])
    return jnp.moveaxis(value.reshape(*before, count, -1, *after), dim, 0)


def sum_at_owner(value, axis, dim):
    pieces = in_blocks(value, dim, lax.axis_size(axis))
    arrived = lax.all_to_all(pieces, axis, split_axis=0, concat_axis=0, tiled=True)
    return arrived.astype(jnp.float32).sum(axis=0)


def split_heads(array):
    length = array.shape[1]
    return array.reshape(2, length, array.shape[2] // DH, DH).transpose(0, 2, 1, 3)


def join_heads(array):
    length = array.shape[2]
    return array.transpose(0, 2, 1, 3).reshape(2, length, array.shape[1] * DH)


def rms_normalize(attended):
    return attended / jnp.sqrt(jnp.mean(attended * attended, axis=-1, keepdims=True) + epsilon)


def add_states(earlier, later):
    return earlier + later


def shards(queries, key_rows, value_rows, out_weight, cotangent):
    head_scale = DH ** (-0.5)
    length = queries.shape[1]
    rows_index = lax.broadcasted_iota(jnp.int32, (length, length), 0)
    cols_index = lax.broadcasted_iota(jnp.int32, (length, length), 1)
    lower = rows_index >= cols_index
    query_heads = split_heads(queries)
    key_heads = split_heads(key_rows)
    value_heads = split_heads(value_rows)
    raw = (
        jnp.einsum("bhtd,bhsd->bhts", query_heads, key_heads, preferred_element_type=jnp.float32)
        * head_scale
    )
    scores = jnp.where(lower, raw, 0.0).astype(jnp.bfloat16)
    local_state = jnp.einsum(
        "bhsd,bhse->bhde", key_heads, value_heads, preferred_element_type=jnp.float32
    )
    state = prefix_by_axis(local_state, CTX, add_states, jnp.zeros_like(local_state), False)
    state_bf = state.astype(jnp.bfloat16)
    attended = jnp.einsum(
        "bhts,bhsd->bhtd", scores, value_heads, preferred_element_type=jnp.float32
    )
    attended = attended + head_scale * jnp.einsum(
        "bhtd,bhde->bhte", query_heads, state_bf, preferred_element_type=jnp.float32
    )
    normed_flat = join_heads(rms_normalize(attended).astype(jnp.bfloat16))
    partial_value = jnp.einsum(
        "btr,rc->btc", normed_flat, out_weight, preferred_element_type=jnp.float32
    )
    layer_output = sum_at_owner(partial_value.astype(jnp.bfloat16), "head", 2).astype(jnp.bfloat16)
    grad_all = lax.all_gather(cotangent, "head", axis=2, tiled=True)
    normed_grad = jnp.einsum(
        "btc,rc->btr", grad_all, out_weight, preferred_element_type=jnp.float32
    )
    weight_term = jnp.einsum(
        "btr,btc->rc", normed_flat, grad_all, preferred_element_type=jnp.float32
    )
    token_factor = (2 * length * lax.axis_size(CTX)) ** (-0.5)
    weight_grad = (
        lax.psum_scatter(
            weight_term.astype(jnp.bfloat16), CTX, scatter_dimension=1, tiled=True
        ).astype(jnp.float32)
        * token_factor
    )
    pullback = jax.vjp(rms_normalize, attended)[1]
    attended_grad = pullback(split_heads(normed_grad))[0].astype(jnp.bfloat16)
    local_grad_state = jnp.einsum(
        "bhtd,bhte->bhde", query_heads, attended_grad, preferred_element_type=jnp.float32
    )
    grad_state = prefix_by_axis(
        local_grad_state, CTX, add_states, jnp.zeros_like(local_grad_state), True
    )
    grad_state_bf = grad_state.astype(jnp.bfloat16)
    raw_grad = (
        jnp.einsum(
            "bhtd,bhsd->bhts", attended_grad, value_heads, preferred_element_type=jnp.float32
        )
        * head_scale
    )
    score_grad = jnp.where(lower, raw_grad, 0.0).astype(jnp.bfloat16)
    query_part = jnp.einsum(
        "bhts,bhsd->bhtd", score_grad, key_heads, preferred_element_type=jnp.float32
    )
    query_part = query_part + head_scale * jnp.einsum(
        "bhte,bhde->bhtd", attended_grad, state_bf, preferred_element_type=jnp.float32
    )
    key_part = jnp.einsum(
        "bhts,bhtd->bhsd", score_grad, query_heads, preferred_element_type=jnp.float32
    )
    key_part = key_part + head_scale * jnp.einsum(
        "bhse,bhde->bhsd", value_heads, grad_state_bf, preferred_element_type=jnp.float32
    )
    value_part = jnp.einsum(
        "bhts,bhte->bhse", scores, attended_grad, preferred_element_type=jnp.float32
    )
    value_part = value_part + head_scale * jnp.einsum(
        "bhsd,bhde->bhse", key_heads, grad_state_bf, preferred_element_type=jnp.float32
    )
    query_grad = join_heads(query_part.astype(jnp.bfloat16))
    key_grad = join_heads(key_part.astype(jnp.bfloat16))
    value_grad = join_heads(value_part.astype(jnp.bfloat16))
    return (layer_output, query_grad, key_grad, value_grad, weight_grad)


def solution(mesh):
    split = Mesh(
        mesh.devices.reshape(4, 4, 2, mesh.shape["head"]), ("ctx_0", "ctx_1", "ctx_2", "head")
    )
    placed = (
        P(None, CTX, "head"),
        P(None, CTX, "head"),
        P(None, CTX, "head"),
        P("head", None),
        P(None, CTX, "head"),
    )
    return jax.shard_map(
        shards,
        mesh=split,
        in_specs=placed,
        out_specs=(
            P(None, CTX, "head"),
            P(None, CTX, "head"),
            P(None, CTX, "head"),
            P(None, CTX, "head"),
            P("head", CTX),
        ),
        check_vma=False,
    )
```

profile of v0, /device:TPU:1, one launch (start us, length us, event | category | flops | bytes accessed | tf_op | source)
XLA Modules:
  0.0 345.1 jit_solution(2595999831184184508)
XLA Ops:
  7.2 0.0 copy-start
  7.2 0.0 all-gather.18.cloned.1.call-start
  7.2 0.9 copy-done
  8.2 2.1 fusion.34
  10.3 0.0 all-gather.18.cloned.1.call-update
  10.3 0.0 all-gather.22.cloned.1.call-start
  10.4 19.0 %all-gather.18.cloned.1.call-done = f32[4,4,128,128]{3,2,1,0:T(8,128)} async-done(((f32[2,4,128,128]{3,2,1,0:T(8,128)}), f32[4,4,128,128]{3,2,1,0:T(8,128)}) %all-gather.18.cloned.1.call-update) | async-done | bytes 1048592 | tf_op jit(solution)/shard_map/all_gather | solution.py:21
  29.4 2.1 slice_add_fusion.13
  31.4 0.0 all-gather.22.cloned.1.call-update
  31.4 0.0 all-gather.14.cloned.1.call-start
  31.5 0.7 all-gather.14.cloned.1.call-update
  32.2 0.0 all-gather.12.cloned.1.call-start
  32.2 33.1 %all-gather.22.cloned.1.call-done = f32[8,4,128,128]{3,2,1,0:T(8,128)} async-done(((f32[2,4,128,128]{3,2,1,0:T(8,128)}), f32[8,4,128,128]{3,2,1,0:T(8,128)}) %all-gather.22.cloned.1.call-update) | async-done | bytes 2097168 | tf_op jit(solution)/shard_map/all_gather | solution.py:21
  65.4 2.4 fusion.31
  67.8 0.0 all-gather.12.cloned.1.call-update
  67.8 0.0 all-gather.20.cloned.1.call-start
  67.9 0.6 copy-done.18
  68.5 1.3 select_convert_fusion.1
  69.8 42.0 %all-gather.14.cloned.1.call-done = bf16[2,192,4096]{2,1,0:T(8,128)(2,1)} async-done(((bf16[2,192,512]{2,1,0:T(8,128)(2,1)}), bf16[2,192,4096]{2,1,0:T(8,128)(2,1)}) %all-gather.14.cloned.1.call-update) | async-done | bytes 3145744 | tf_op jit(solution)/shard_map/all_gather | solution.py:90
  111.8 5.9 %fusion.3 = f32[2,24,4,8,128]{4,3,2,1,0:T(8,128)} fusion(bf16[2,192,4096]{2,1,0:T(8,128)(2,1)} %all-gather.14.cloned.1.call-done, bf16[512,4096]{1,0:T(8,128)(2,1)} %param.8), kind=kOutput, calls=%fused_computation.8 | convolution fusion | flops 1610612736 | bytes 8126464 | tf_op jit(solution)/shard_map/btc,rc->btr/dot_general | solution.py:91
  117.7 28.1 %all-gather.12.cloned.1.call-done = f32[4,2,4,128,128]{4,3,2,1,0:T(8,128)} async-done(((f32[1,2,4,128,128]{4,3,2,1,0:T(8,128)}), f32[4,2,4,128,128]{4,3,2,1,0:T(8,128)}) %all-gather.12.cloned.1.call-update) | async-done | bytes 2097168 | tf_op jit(solution)/shard_map/all_gather | solution.py:21
  145.8 2.2 fusion.30
  148.0 0.3 convolution_multiply_fusion.1
  148.3 0.5 multiply_reduce_fusion
  148.9 0.4 copy-done.15
  149.2 0.6 fusion.21
  149.9 0.5 fusion.17
  150.4 0.7 copy-done.2
  151.2 0.3 convolution_bitcast_fusion.2
  151.5 1.0 copy.35
  152.5 0.0 all-gather.20.cloned.1.call-update
  152.5 0.0 all-gather.24.cloned.1.call-start
  152.6 15.4 %all-gather.20.cloned.1.call-done = f32[4,4,128,128]{3,2,1,0:T(8,128)} async-done(((f32[2,4,128,128]{3,2,1,0:T(8,128)}), f32[4,4,128,128]{3,2,1,0:T(8,128)}) %all-gather.20.cloned.1.call-update) | async-done | bytes 1048592 | tf_op jit(solution)/shard_map/all_gather | solution.py:21
  168.0 2.1 slice_add_fusion.6
  170.1 0.0 all-gather.24.cloned.1.call-update
  170.1 0.0 reduce-scatter.4.cloned.1.call-start
  170.1 0.3 fusion.37
  170.4 6.3 %bitcast_convert_fusion = bf16[512,4096]{1,0:T(8,128)(2,1)} fusion(bf16[2,192,4096]{2,1,0:T(8,128)(2,1)} %all-gather.14.cloned.1.call-done, bf16[2,4,24,8,128]{4,3,2,1,0:T(8,128)(2,1)S(1)} %fusion.37), kind=kOutput, calls=%fused_computation | convolution fusion | flops 1612709888 | bytes 7733248 | tf_op jit(solution)/shard_map/btr,btc->rc/dot_general | solution.py:94
  176.7 6.5 %copy.41 = bf16[512,4096]{0,1:T(8,128)(2,1)} copy(bf16[512,4096]{1,0:T(8,128)(2,1)} %bitcast_convert_fusion) | data formatting | bytes 8388608
  183.2 0.0 reduce-scatter.4.cloned.1.call-update
  183.2 4.2 %convolution_convert_fusion = bf16[2,192,4096]{2,1,0:T(8,128)(2,1)S(1)} fusion(bf16[512,4096]{1,0:T(8,128)(2,1)} %param.8, bf16[2,4,24,8,128]{4,3,2,1,0:T(8,128)(2,1)S(1)} %fusion.37), kind=kOutput, calls=%fused_computation.1 | convolution fusion | flops 1612185600 | bytes 7733248 | tf_op jit(solution)/shard_map/btr,rc->btc/dot_general | solution.py:86
  187.4 2.0 copy.116
  189.4 6.5 %all-to-all-start = ((bf16[8,2,192,512]{3,2,1,0:T(8,128)(2,1)}), bf16[8,2,192,512]{3,2,1,0:T(8,128)(2,1)S(1)}, u32[]{:S(2)}, u32[]{:S(2)}) async-start(bf16[8,2,192,512]{3,2,1,0:T(8,128)(2,1)} %bitcast.230), calls=%async_computation | async-start | bytes 6291456 | tf_op jit(solution)/shard_map/all_to_all | solution.py:38
  195.9 0.2 all-gather.16.cloned.1.call-start
  196.1 7.8 %all-gather.24.cloned.1.call-done = f32[8,4,128,128]{3,2,1,0:T(8,128)} async-done(((f32[2,4,128,128]{3,2,1,0:T(8,128)}), f32[8,4,128,128]{3,2,1,0:T(8,128)}) %all-gather.24.cloned.1.call-update) | async-done | bytes 2097168 | tf_op jit(solution)/shard_map/all_gather | solution.py:21
  204.0 2.4 fusion.27
  206.4 0.0 all-gather.16.cloned.1.call-update
  206.5 1.5 select_convert_fusion
  208.0 1.6 fusion.36
  209.6 0.3 fusion.16
  209.9 0.8 copy.117
  210.7 59.5 %all-to-all-done = bf16[8,2,192,512]{3,2,1,0:T(8,128)(2,1)S(1)} async-done(((bf16[8,2,192,512]{3,2,1,0:T(8,128)(2,1)}), bf16[8,2,192,512]{3,2,1,0:T(8,128)(2,1)S(1)}, u32[]{:S(2)}, u32[]{:S(2)}) %all-to-all-start) | async-done | bytes 3145760 | tf_op jit(solution)/shard_map/all_to_all | solution.py:38
  270.2 1.3 reduce_sum.34
  271.5 24.9 %reduce-scatter.4.cloned.1.call-done = bf16[128,512]{1,0:T(8,128)(2,1)} async-done(((bf16[4096,512]{1,0:T(8,128)(2,1)}), bf16[128,512]{1,0:T(8,128)(2,1)}) %reduce-scatter.4.cloned.1.call-update) | async-done | bytes 131088
  296.4 1.0 copy.42
  297.4 0.7 convert_multiply_fusion
  298.2 34.4 %all-gather.16.cloned.1.call-done = f32[4,2,4,128,128]{4,3,2,1,0:T(8,128)} async-done(((f32[1,2,4,128,128]{4,3,2,1,0:T(8,128)}), f32[4,2,4,128,128]{4,3,2,1,0:T(8,128)}) %all-gather.16.cloned.1.call-update) | async-done | bytes 2097168 | tf_op jit(solution)/shard_map/all_gather | solution.py:21
  332.5 3.0 fusion.26
  335.6 0.3 fusion.6
  335.8 0.3 fusion.7
  336.2 0.5 fusion.15
  336.6 0.2 copy-done.14
  336.8 0.5 fusion.14
  337.3 1.0 copy_bitcast_fusion
  (35 shorter events, 0.1 us)
Async XLA Ops:
  7.2 1.0 copy-start
  7.2 22.2 %all-gather.18.cloned.1.call-start = ((), (), s32[]{:S(2)}) async-start(), calls=%async_computation.5 | async-start | bytes 1572864 | tf_op jit(solution)/shard_map/all_gather | solution.py:21
  10.3 58.2 %copy-start.6 = (bf16[2,192,512]{2,1,0:T(8,128)(2,1)S(1)}, bf16[2,192,512]{2,1,0:T(8,128)(2,1)}, u32[]{:S(2)}) copy-start(bf16[2,192,512]{2,1,0:T(8,128)(2,1)} %param.5) | copy-start | bytes 1179652
  10.3 58.2 %copy-start.9 = (bf16[2,192,512]{2,1,0:T(8,128)(2,1)S(1)}, bf16[2,192,512]{2,1,0:T(8,128)(2,1)}, u32[]{:S(2)}) copy-start(bf16[2,192,512]{2,1,0:T(8,128)(2,1)} %param.6) | copy-start | bytes 1179652
  10.3 55.0 %all-gather.22.cloned.1.call-start = ((), (), s32[]{:S(2)}) async-start(), calls=%async_computation.7 | async-start | bytes 2621440 | tf_op jit(solution)/shard_map/all_gather | solution.py:21
  31.4 80.4 %all-gather.14.cloned.1.call-start = ((), (), s32[]{:S(2)}) async-start(), calls=%async_computation.3 | async-start | bytes 3538944 | tf_op jit(solution)/shard_map/all_gather | solution.py:90
  32.2 113.6 %all-gather.12.cloned.1.call-start = ((), (), s32[]{:S(2)}) async-start(), calls=%async_computation.2 | async-start | bytes 2621440 | tf_op jit(solution)/shard_map/all_gather | solution.py:21
  67.8 100.2 %all-gather.20.cloned.1.call-start = ((), (), s32[]{:S(2)}) async-start(), calls=%async_computation.6 | async-start | bytes 1572864 | tf_op jit(solution)/shard_map/all_gather | solution.py:21
  67.9 0.6 copy-start.18
  69.8 76.0 %copy-start.1 = (f32[8,4,128,128]{3,2,1,0:T(8,128)S(1)}, f32[8,4,128,128]{3,2,1,0:T(8,128)}, u32[]{:S(2)}) copy-start(f32[8,4,128,128]{3,2,1,0:T(8,128)} %all-gather.22.cloned.1.call-done) | copy-start | bytes 6291460
  69.8 76.0 %copy-start.5 = (f32[4,4,128,128]{3,2,1,0:T(8,128)S(1)}, f32[4,4,128,128]{3,2,1,0:T(8,128)}, u32[]{:S(2)}) copy-start(f32[4,4,128,128]{3,2,1,0:T(8,128)} %all-gather.18.cloned.1.call-done) | copy-start | bytes 3145732
  145.8 2.2 copy-start.7
  145.8 2.5 copy-start.11
  148.0 1.9 copy-start.16
  148.0 1.2 copy-start.15
  150.4 0.7 copy-start.2
  152.5 51.5 %all-gather.24.cloned.1.call-start = ((), (), s32[]{:S(2)}) async-start(), calls=%async_computation.8 | async-start | bytes 2621440 | tf_op jit(solution)/shard_map/all_gather | solution.py:21
  170.1 126.3 %reduce-scatter.4.cloned.1.call-start = ((), (), s32[]{:S(2)}) async-start(), calls=%async_computation.9 | async-start | bytes 4325376
  189.4 80.8 %all-to-all-start = ((bf16[8,2,192,512]{3,2,1,0:T(8,128)(2,1)}), bf16[8,2,192,512]{3,2,1,0:T(8,128)(2,1)S(1)}, u32[]{:S(2)}, u32[]{:S(2)}) async-start(bf16[8,2,192,512]{3,2,1,0:T(8,128)(2,1)} %bitcast.230), calls=%async_computation | async-start | bytes 6291456 | tf_op jit(solution)/shard_map/all_to_all | solution.py:38
  195.9 136.6 %all-gather.16.cloned.1.call-start = ((), (), s32[]{:S(2)}) async-start(), calls=%async_computation.4 | async-start | bytes 2621440 | tf_op jit(solution)/shard_map/all_gather | solution.py:21
  206.5 3.1 copy-start.3
  206.5 3.1 copy-start.17
  207.9 2.0 copy-start.13
  271.5 64.1 %copy-start.10 = (bf16[2,192,512]{2,1,0:T(8,128)(2,1)S(1)}, bf16[2,192,512]{2,1,0:T(8,128)(2,1)}, u32[]{:S(2)}) copy-start(bf16[2,192,512]{2,1,0:T(8,128)(2,1)} %param.6) | copy-start | bytes 1179652
  298.2 38.0 %copy-start.4 = (bf16[2,4,192,128]{3,2,1,0:T(8,128)(2,1)S(1)}, bf16[2,4,192,128]{3,2,1,0:T(8,128)(2,1)}, u32[]{:S(2)}) copy-start(bf16[2,4,192,128]{3,2,1,0:T(8,128)(2,1)} %copy-done.2) | copy-start | bytes 1179652
  298.2 38.0 %copy-start.12 = (bf16[2,4,192,192]{3,2,1,0:T(8,128)(2,1)S(1)}, bf16[2,4,192,192]{3,2,1,0:T(8,128)(2,1)}, u32[]{:S(2)}) copy-start(bf16[2,4,192,192]{3,2,1,0:T(8,128)(2,1)} %select_convert_fusion.1) | copy-start | bytes 1769476
  335.6 1.1 copy-start.8
  335.6 1.2 copy-start.14
Sparse Core Ops, SparseCore 0:
  10.5 18.8 all-gather.17
  31.6 33.7 all-gather.21
  67.2 44.6 all-gather.13
  113.5 32.3 all-gather.11
  152.7 15.3 all-gather.19
  170.2 33.7 all-gather.23
  207.9 88.4 reduce-scatter.3
  298.2 34.2 all-gather.15
where the time goes:
time: 346 us; the launch traced here: 345 us
  waiting for transfers between devices  265 us (77%)
  matrix products  25.8 us (7%)
  other arithmetic  17.6 us (5%)
  local copies, waits for them, and re-layouts  15.2 us (4%)
  between operations  14.5 us (4%)
  starting transfers between devices  7.02 us (2%)
    all_gather x6, waiting for transfers between devices, prefix_by_axis(): pieces = lax.all_gather(subtotal, axis)  138 us
    all_to_all x1, waiting for transfers between devices, sum_at_owner(): lax.all_to_all(pieces, axis, split_axis=0, concat_axis=0, tiled=True)  59.5 us
    all_gather x1, waiting for transfers between devices, shards(): grad_all = lax.all_gather(cotangent, 'head', axis=2, tiled=True)  42 us
    unnamed x9, waiting for transfers between devices  25.7 us
    unnamed x40, local copies, waits for them, and re-layouts  10.4 us
    add x4, other arithmetic, add_states(): return earlier + later  8.94 us
  transfers between devices with their start and end apart: 9, of which 9 were waited for; matrix products, arithmetic and copies ran while one was open for 11% of the time, Pallas kernels for 0%

commit v1 on v0

--- a/solution.py
+++ b/solution.py
@@ -87,7 +87,16 @@
         "btr,rc->btc", normed_flat, out_weight, preferred_element_type=jnp.float32
     )
     layer_output = sum_at_owner(partial_value.astype(jnp.bfloat16), "head", 2).astype(jnp.bfloat16)
-    grad_all = lax.all_gather(cotangent, "head", axis=2, tiled=True)
+    ways = lax.axis_size("head")
+    up = [(d, (d + 1) % ways) for d in range(ways)]
+    down = [(d, (d - 1) % ways) for d in range(ways)]
+    earlier_2, later_2 = ([cotangent], [cotangent])
+    for _ in range(ways // 2):
+        earlier_2.append(lax.ppermute(earlier_2[-1], "head", up))
+    for _ in range((ways - 1) // 2):
+        later_2.append(lax.ppermute(later_2[-1], "head", down))
+    line = jnp.concatenate([*earlier_2[::-1], *later_2[1:]], axis=2)
+    grad_all = jnp.roll(line, (lax.axis_index("head") - ways // 2) * cotangent.shape[2], axis=2)
     normed_grad = jnp.einsum(
         "btc,rc->btr", grad_all, out_weight, preferred_element_type=jnp.float32
     )

time: 346 us -> 302 us (0.87)
  waiting for transfers between devices: 265 us -> 207 us
  starting transfers between devices: 7.02 us -> 17.2 us
  local copies, waits for them, and re-layouts: 15.2 us -> 19.8 us
    all_gather x6, waiting for transfers between devices: 138 us -> 92.4 us  [prefix_by_axis(): pieces = lax.all_gather(subtotal, axis)]
    all_gather x1 -> x0, waiting for transfers between devices: 42 us -> none  [shards(): grad_all = lax.all_gather(cotangent, 'head', axis=2, tiled=True)]
    ppermute x0 -> x7, waiting for transfers between devices: none -> 31.1 us  [the longest x4 19.4 us: shards(): earlier_2.append(lax.ppermute(earlier_2[-1], 'head', up))]
    ppermute x0 -> x7, starting transfers between devices: none -> 10.3 us  [the longest x3 9.19 us: shards(): later_2.append(lax.ppermute(later_2[-1], 'head', down))]
    unnamed x40 -> x57, local copies, waits for them, and re-layouts: 10.4 us -> 15 us
    unnamed x9 -> x8, waiting for transfers between devices: 25.7 us -> 24.7 us
  transfers between devices with their start and end apart: 9 -> 15, of which waited for: 9 -> 12; matrix products, arithmetic and copies ran while one was open for 11% -> 13% of each run, Pallas kernels for 0% -> 0%
where the time goes in v1:
time: 302 us; the launch traced here: 301 us
  waiting for transfers between devices  207 us (69%)
  matrix products  24.8 us (8%)
  local copies, waits for them, and re-layouts  19.8 us (7%)
  other arithmetic  17.7 us (6%)
  starting transfers between devices  17.2 us (6%)
  between operations  14.6 us (5%)
    all_gather x6, waiting for transfers between devices, prefix_by_axis(): pieces = lax.all_gather(subtotal, axis)  92.4 us
    all_to_all x1, waiting for transfers between devices, sum_at_owner(): lax.all_to_all(pieces, axis, split_axis=0, concat_axis=0, tiled=True)  58.7 us
    unnamed x8, waiting for transfers between devices  24.7 us
    ppermute x4, waiting for transfers between devices, shards(): earlier_2.append(lax.ppermute(earlier_2[-1], 'head', up))  19.4 us
    unnamed x57, local copies, waits for them, and re-layouts  15 us
    ppermute x3, waiting for transfers between devices, shards(): later_2.append(lax.ppermute(later_2[-1], 'head', down))  11.7 us
    ppermute x3, starting transfers between devices, shards(): later_2.append(lax.ppermute(later_2[-1], 'head', down))  9.19 us
    add x4, other arithmetic, add_states(): return earlier + later  9.01 us
  transfers between devices with their start and end apart: 15, of which 12 were waited for; matrix products, arithmetic and copies ran while one was open for 13% of the time, Pallas kernels for 0%

profile of v1, /device:TPU:1, one launch (start us, length us, event | category | flops | bytes accessed | tf_op | source)
XLA Modules:
  0.0 301.1 jit_solution(17429279098058415954)
XLA Ops:
  7.2 0.0 all-gather.15.cloned.1.call-start
  7.3 0.9 copy-done
  8.2 2.1 fusion.38
  10.3 0.0 all-gather.19.cloned.1.call-start
  10.4 19.0 %all-gather.15.cloned.1.call-done = f32[4,4,128,128]{3,2,1,0:T(8,128)} async-done(((f32[2,4,128,128]{3,2,1,0:T(8,128)}), f32[4,4,128,128]{3,2,1,0:T(8,128)}) %all-gather.15.cloned.1.call-update) | async-done | bytes 1048592 | tf_op jit(solution)/shard_map/all_gather | solution.py:21
  29.3 2.1 slice_add_fusion.13
  31.4 0.0 all-gather.19.cloned.1.call-update
  31.5 0.0 all-gather.11.cloned.1.call-start
  31.5 1.1 collective-permute-start
  32.6 11.1 %collective-permute-done = bf16[2,192,512]{2,1,0:T(8,128)(2,1)S(1)} collective-permute-done((bf16[2,192,512]{2,1,0:T(8,128)(2,1)}, bf16[2,192,512]{2,1,0:T(8,128)(2,1)S(1)}, u32[]{:S(2)}, u32[]{:S(2)}) %collective-permute-start) | collective-permute-done | bytes 393248 | tf_op jit(solution)/shard_map/ppermute | solution.py:95
  43.7 2.7 collective-permute-start.4
  46.3 8.3 %collective-permute-done.1 = bf16[2,192,512]{2,1,0:T(8,128)(2,1)S(1)} collective-permute-done((bf16[2,192,512]{2,1,0:T(8,128)(2,1)S(1)}, bf16[2,192,512]{2,1,0:T(8,128)(2,1)S(1)}, u32[]{:S(2)}, u32[]{:S(2)}) %collective-permute-start.1) | collective-permute-done | bytes 393248 | tf_op jit(solution)/shard_map/ppermute | solution.py:95
  54.7 10.7 %all-gather.19.cloned.1.call-done = f32[8,4,128,128]{3,2,1,0:T(8,128)} async-done(((f32[2,4,128,128]{3,2,1,0:T(8,128)}), f32[8,4,128,128]{3,2,1,0:T(8,128)}) %all-gather.19.cloned.1.call-update) | async-done | bytes 2097168 | tf_op jit(solution)/shard_map/all_gather | solution.py:21
  65.4 2.5 fusion.35
  67.8 0.0 all-gather.11.cloned.1.call-update
  67.9 0.0 all-gather.17.cloned.1.call-start
  67.9 3.1 %collective-permute-start.5 = (bf16[2,192,512]{2,1,0:T(8,128)(2,1)S(1)}, bf16[2,192,512]{2,1,0:T(8,128)(2,1)S(1)}, u32[]{:S(2)}, u32[]{:S(2)}) collective-permute-start(bf16[2,192,512]{2,1,0:T(8,128)(2,1)S(1)} %collective-permute-done.4), channel_id=1, source_target_pairs={{0,7},{1,0},{2,1},{3,2},{4,3},{5,4},{6,5},{7,6},{8,15},{9,8},{10,9... | collective-permute-start | bytes 1179656 | tf_op jit(solution)/shard_map/ppermute | solution.py:97
  71.1 1.3 select_convert_fusion.1
  72.4 6.3 %collective-permute-done.5 = bf16[2,192,512]{2,1,0:T(8,128)(2,1)S(1)} collective-permute-done((bf16[2,192,512]{2,1,0:T(8,128)(2,1)S(1)}, bf16[2,192,512]{2,1,0:T(8,128)(2,1)S(1)}, u32[]{:S(2)}, u32[]{:S(2)}) %collective-permute-start.5) | collective-permute-done | bytes 393248 | tf_op jit(solution)/shard_map/ppermute | solution.py:97
  78.7 3.4 %collective-permute-start.6 = (bf16[2,192,512]{2,1,0:T(8,128)(2,1)S(1)}, bf16[2,192,512]{2,1,0:T(8,128)(2,1)S(1)}, u32[]{:S(2)}, u32[]{:S(2)}) collective-permute-start(bf16[2,192,512]{2,1,0:T(8,128)(2,1)S(1)} %collective-permute-done.5), channel_id=1, source_target_pairs={{0,7},{1,0},{2,1},{3,2},{4,3},{5,4},{6,5},{7,6},{8,15},{9,8},{10,9... | collective-permute-start | bytes 1179656 | tf_op jit(solution)/shard_map/ppermute | solution.py:97
  82.1 1.0 constant_dynamic-update-slice_fusion.15
  83.4 5.4 %collective-permute-done.6 = bf16[2,192,512]{2,1,0:T(8,128)(2,1)S(1)} collective-permute-done((bf16[2,192,512]{2,1,0:T(8,128)(2,1)S(1)}, bf16[2,192,512]{2,1,0:T(8,128)(2,1)S(1)}, u32[]{:S(2)}, u32[]{:S(2)}) %collective-permute-start.6) | collective-permute-done | bytes 393248 | tf_op jit(solution)/shard_map/ppermute | solution.py:97
  88.9 1.0 constant_dynamic-update-slice_fusion.7
  90.3 3.2 %copy-done.16 = bf16[2,192,8192]{2,1,0:T(8,128)(2,1)} copy-done((bf16[2,192,8192]{2,1,0:T(8,128)(2,1)}, bf16[2,192,8192]{2,1,0:T(8,128)(2,1)S(1)}, u32[]{:S(2)}) %copy-start.16) | copy-done | bytes 6291480
  93.5 2.7 fusion.5
  96.2 5.1 %all-gather.11.cloned.1.call-done = f32[4,2,4,128,128]{4,3,2,1,0:T(8,128)} async-done(((f32[1,2,4,128,128]{4,3,2,1,0:T(8,128)}), f32[4,2,4,128,128]{4,3,2,1,0:T(8,128)}) %all-gather.11.cloned.1.call-update) | async-done | bytes 2097168 | tf_op jit(solution)/shard_map/all_gather | solution.py:21
  101.4 2.2 fusion.34
  103.6 1.3 convolution_multiply_fusion.1
  105.0 0.5 multiply_reduce_fusion
  105.5 0.6 fusion.25
  106.2 0.5 fusion.21
  106.7 0.7 copy-done.2
  107.4 0.3 convolution_bitcast_fusion.2
  107.8 1.0 copy.35
  108.8 0.0 all-gather.17.cloned.1.call-update
  108.8 0.0 all-gather.21.cloned.1.call-start
  108.9 15.4 %all-gather.17.cloned.1.call-done = f32[4,4,128,128]{3,2,1,0:T(8,128)} async-done(((f32[2,4,128,128]{3,2,1,0:T(8,128)}), f32[4,4,128,128]{3,2,1,0:T(8,128)}) %all-gather.17.cloned.1.call-update) | async-done | bytes 1048592 | tf_op jit(solution)/shard_map/all_gather | solution.py:21
  124.3 2.0 slice_add_fusion.6
  126.3 0.2 reduce-scatter.4.cloned.1.call-start
  126.6 0.3 fusion.41
  126.9 6.4 %bitcast_convert_fusion = bf16[512,4096]{1,0:T(8,128)(2,1)} fusion(bf16[2,192,8192]{2,1,0:T(8,128)(2,1)} %copy-done.16, s32[]{:T(128)S(6)} %select_n.199, bf16[2,4,24,8,128]{4,3,2,1,0:T(8,128)(2,1)S(1)} %fusion.41), kind=kOutput, calls=%fused_computation | convolution fusion | flops 1612709888 | bytes 7733252 | tf_op jit(solution)/shard_map/btr,btc->rc/dot_general | solution.py:103
  133.2 6.5 %copy.41 = bf16[512,4096]{0,1:T(8,128)(2,1)} copy(bf16[512,4096]{1,0:T(8,128)(2,1)} %bitcast_convert_fusion) | data formatting | bytes 8388608
  139.7 4.2 %convolution_convert_fusion = bf16[2,192,4096]{2,1,0:T(8,128)(2,1)S(1)} fusion(bf16[512,4096]{1,0:T(8,128)(2,1)} %param.8, bf16[2,4,24,8,128]{4,3,2,1,0:T(8,128)(2,1)S(1)} %fusion.41), kind=kOutput, calls=%fused_computation.1 | convolution fusion | flops 1612185600 | bytes 7733248 | tf_op jit(solution)/shard_map/btr,rc->btc/dot_general | solution.py:86
  143.9 2.0 copy.116
  145.9 6.5 %all-to-all-start = ((bf16[8,2,192,512]{3,2,1,0:T(8,128)(2,1)}), bf16[8,2,192,512]{3,2,1,0:T(8,128)(2,1)S(1)}, u32[]{:S(2)}, u32[]{:S(2)}) async-start(bf16[8,2,192,512]{3,2,1,0:T(8,128)(2,1)} %bitcast.228), calls=%async_computation | async-start | bytes 6291456 | tf_op jit(solution)/shard_map/all_to_all | solution.py:38
  152.4 0.0 all-gather.13.cloned.1.call-start
  152.4 7.8 %all-gather.21.cloned.1.call-done = f32[8,4,128,128]{3,2,1,0:T(8,128)} async-done(((f32[2,4,128,128]{3,2,1,0:T(8,128)}), f32[8,4,128,128]{3,2,1,0:T(8,128)}) %all-gather.21.cloned.1.call-update) | async-done | bytes 2097168 | tf_op jit(solution)/shard_map/all_gather | solution.py:21
  160.3 2.4 fusion.31
  162.7 1.4 select_convert_fusion
  164.1 1.6 fusion.40
  165.8 1.4 fusion.20
  167.2 0.8 copy.117
  168.0 58.7 %all-to-all-done = bf16[8,2,192,512]{3,2,1,0:T(8,128)(2,1)S(1)} async-done(((bf16[8,2,192,512]{3,2,1,0:T(8,128)(2,1)}), bf16[8,2,192,512]{3,2,1,0:T(8,128)(2,1)S(1)}, u32[]{:S(2)}, u32[]{:S(2)}) %all-to-all-start) | async-done | bytes 3145760 | tf_op jit(solution)/shard_map/all_to_all | solution.py:38
  226.7 1.3 reduce_sum.34
  228.0 24.6 %reduce-scatter.4.cloned.1.call-done = bf16[128,512]{1,0:T(8,128)(2,1)} async-done(((bf16[4096,512]{1,0:T(8,128)(2,1)}), bf16[128,512]{1,0:T(8,128)(2,1)}) %reduce-scatter.4.cloned.1.call-update) | async-done | bytes 131088
  252.6 1.0 copy.42
  253.6 0.7 convert_multiply_fusion
  254.3 34.3 %all-gather.13.cloned.1.call-done = f32[4,2,4,128,128]{4,3,2,1,0:T(8,128)} async-done(((f32[1,2,4,128,128]{4,3,2,1,0:T(8,128)}), f32[4,2,4,128,128]{4,3,2,1,0:T(8,128)}) %all-gather.13.cloned.1.call-update) | async-done | bytes 2097168 | tf_op jit(solution)/shard_map/all_gather | solution.py:21
  288.7 3.0 fusion.30
  291.7 0.3 fusion.11
  292.0 0.3 fusion.10
  292.3 0.5 fusion.18
  292.8 0.5 fusion.19
  293.2 1.0 copy_bitcast_fusion
  (64 shorter events, 0.8 us)
Async XLA Ops:
  7.2 1.0 copy-start
  7.2 63.9 %copy-start.8 = (bf16[2,192,512]{2,1,0:T(8,128)(2,1)S(1)}, bf16[2,192,512]{2,1,0:T(8,128)(2,1)}, u32[]{:S(2)}) copy-start(bf16[2,192,512]{2,1,0:T(8,128)(2,1)} %param.6) | copy-start | bytes 1179652
  7.2 76.1 %copy-start.17 = (bf16[2,192,512]{2,1,0:T(8,128)(2,1)S(1)}, bf16[2,192,512]{2,1,0:T(8,128)(2,1)}, u32[]{:S(2)}) copy-start(bf16[2,192,512]{2,1,0:T(8,128)(2,1)} %param.9) | copy-start | bytes 1179652
  7.2 63.9 %copy-start.5 = (bf16[2,192,512]{2,1,0:T(8,128)(2,1)S(1)}, bf16[2,192,512]{2,1,0:T(8,128)(2,1)}, u32[]{:S(2)}) copy-start(bf16[2,192,512]{2,1,0:T(8,128)(2,1)} %param.5) | copy-start | bytes 1179652
  7.2 22.1 %all-gather.15.cloned.1.call-start = ((), (), s32[]{:S(2)}) async-start(), calls=%async_computation.4 | async-start | bytes 1572864 | tf_op jit(solution)/shard_map/all_gather | solution.py:21
  10.3 55.1 %all-gather.19.cloned.1.call-start = ((), (), s32[]{:S(2)}) async-start(), calls=%async_computation.6 | async-start | bytes 2621440 | tf_op jit(solution)/shard_map/all_gather | solution.py:21
  31.5 69.9 %all-gather.11.cloned.1.call-start = ((), (), s32[]{:S(2)}) async-start(), calls=%async_computation.2 | async-start | bytes 2621440 | tf_op jit(solution)/shard_map/all_gather | solution.py:21
  31.5 12.2 %collective-permute-start = (bf16[2,192,512]{2,1,0:T(8,128)(2,1)}, bf16[2,192,512]{2,1,0:T(8,128)(2,1)S(1)}, u32[]{:S(2)}, u32[]{:S(2)}) collective-permute-start(bf16[2,192,512]{2,1,0:T(8,128)(2,1)} %param.9), channel_id=1, source_target_pairs={{0,1},{1,2},{2,3},{3,4},{4,5},{5,6},{6,7},{7,0},{8,9},{9,10},{10,1... | collective-permute-start | bytes 1179656 | tf_op jit(solution)/shard_map/ppermute | solution.py:95
  43.7 11.0 %collective-permute-start.1 = (bf16[2,192,512]{2,1,0:T(8,128)(2,1)S(1)}, bf16[2,192,512]{2,1,0:T(8,128)(2,1)S(1)}, u32[]{:S(2)}, u32[]{:S(2)}) collective-permute-start(bf16[2,192,512]{2,1,0:T(8,128)(2,1)S(1)} %collective-permute-done), channel_id=1, source_target_pairs={{0,1},{1,2},{2,3},{3,4},{4,5},{5,6},{6,7},{7,0},{8,9},{9,10},{10,1... | collective-permute-start | bytes 1179656 | tf_op jit(solution)/shard_map/ppermute | solution.py:95
  43.7 24.3 %collective-permute-start.4 = (bf16[2,192,512]{2,1,0:T(8,128)(2,1)}, bf16[2,192,512]{2,1,0:T(8,128)(2,1)S(1)}, u32[]{:S(2)}, u32[]{:S(2)}) collective-permute-start(bf16[2,192,512]{2,1,0:T(8,128)(2,1)} %param.9), channel_id=1, source_target_pairs={{0,7},{1,0},{2,1},{3,2},{4,3},{5,4},{6,5},{7,6},{8,15},{9,8},{10,9... | collective-permute-start | bytes 1179656 | tf_op jit(solution)/shard_map/ppermute | solution.py:97
  54.7 16.4 %collective-permute-start.2 = (bf16[2,192,512]{2,1,0:T(8,128)(2,1)S(1)}, bf16[2,192,512]{2,1,0:T(8,128)(2,1)S(1)}, u32[]{:S(2)}, u32[]{:S(2)}) collective-permute-start(bf16[2,192,512]{2,1,0:T(8,128)(2,1)S(1)} %collective-permute-done.1), channel_id=1, source_target_pairs={{0,1},{1,2},{2,3},{3,4},{4,5},{5,6},{6,7},{7,0},{8,9},{9,10},{10,1... | collective-permute-start | bytes 1179656 | tf_op jit(solution)/shard_map/ppermute | solution.py:95
  67.9 56.4 %all-gather.17.cloned.1.call-start = ((), (), s32[]{:S(2)}) async-start(), calls=%async_computation.5 | async-start | bytes 1572864 | tf_op jit(solution)/shard_map/all_gather | solution.py:21
  67.9 10.7 %collective-permute-start.5 = (bf16[2,192,512]{2,1,0:T(8,128)(2,1)S(1)}, bf16[2,192,512]{2,1,0:T(8,128)(2,1)S(1)}, u32[]{:S(2)}, u32[]{:S(2)}) collective-permute-start(bf16[2,192,512]{2,1,0:T(8,128)(2,1)S(1)} %collective-permute-done.4), channel_id=1, source_target_pairs={{0,7},{1,0},{2,1},{3,2},{4,3},{5,4},{6,5},{7,6},{8,15},{9,8},{10,9... | collective-permute-start | bytes 1179656 | tf_op jit(solution)/shard_map/ppermute | solution.py:97
  71.0 11.0 %collective-permute-start.3 = (bf16[2,192,512]{2,1,0:T(8,128)(2,1)S(1)}, bf16[2,192,512]{2,1,0:T(8,128)(2,1)}, u32[]{:S(2)}, u32[]{:S(2)}) collective-permute-start(bf16[2,192,512]{2,1,0:T(8,128)(2,1)S(1)} %collective-permute-done.2), channel_id=1, source_target_pairs={{0,1},{1,2},{2,3},{3,4},{4,5},{5,6},{6,7},{7,0},{8,9},{9,10},{10,1... | collective-permute-start | bytes 1179656 | tf_op jit(solution)/shard_map/ppermute | solution.py:95
  71.1 19.1 %copy-start.18 = (pred[192,192]{1,0:T(8,128)(4,1)}, pred[192,192]{1,0:T(8,128)(4,1)S(1)}, u32[]{:S(2)}) copy-start(pred[192,192]{1,0:T(8,128)(4,1)S(1)} %iota_compare_fusion) | copy-start | bytes 110596
  72.4 21.1 %copy-start.19 = (bf16[512,4096]{1,0:T(8,128)(2,1)S(1)}, bf16[512,4096]{1,0:T(8,128)(2,1)}, u32[]{:S(2)}) copy-start(bf16[512,4096]{1,0:T(8,128)(2,1)} %param.8) | copy-start | bytes 12582916
  78.7 10.2 %collective-permute-start.6 = (bf16[2,192,512]{2,1,0:T(8,128)(2,1)S(1)}, bf16[2,192,512]{2,1,0:T(8,128)(2,1)S(1)}, u32[]{:S(2)}, u32[]{:S(2)}) collective-permute-start(bf16[2,192,512]{2,1,0:T(8,128)(2,1)S(1)} %collective-permute-done.5), channel_id=1, source_target_pairs={{0,7},{1,0},{2,1},{3,2},{4,3},{5,4},{6,5},{7,6},{8,15},{9,8},{10,9... | collective-permute-start | bytes 1179656 | tf_op jit(solution)/shard_map/ppermute | solution.py:97
  90.3 11.1 %copy-start.1 = (f32[8,4,128,128]{3,2,1,0:T(8,128)S(1)}, f32[8,4,128,128]{3,2,1,0:T(8,128)}, u32[]{:S(2)}) copy-start(f32[8,4,128,128]{3,2,1,0:T(8,128)} %all-gather.19.cloned.1.call-done) | copy-start | bytes 6291460
  90.3 11.1 %copy-start.4 = (f32[4,4,128,128]{3,2,1,0:T(8,128)S(1)}, f32[4,4,128,128]{3,2,1,0:T(8,128)}, u32[]{:S(2)}) copy-start(f32[4,4,128,128]{3,2,1,0:T(8,128)} %all-gather.15.cloned.1.call-done) | copy-start | bytes 3145732
  90.3 3.2 %copy-start.16 = (bf16[2,192,8192]{2,1,0:T(8,128)(2,1)}, bf16[2,192,8192]{2,1,0:T(8,128)(2,1)S(1)}, u32[]{:S(2)}) copy-start(bf16[2,192,8192]{2,1,0:T(8,128)(2,1)S(1)} %constant_dynamic-update-slice_fusion) | copy-start | bytes 18874372
  101.4 3.6 %copy-start.10 = (bf16[2,4,192,192]{3,2,1,0:T(8,128)(2,1)S(1)}, bf16[2,4,192,192]{3,2,1,0:T(8,128)(2,1)}, u32[]{:S(2)}) copy-start(bf16[2,4,192,192]{3,2,1,0:T(8,128)(2,1)} %select_convert_fusion.1) | copy-start | bytes 1769476
  101.4 4.1 %copy-start.14 = (f32[2,24,4,8,128]{4,3,2,1,0:T(8,128)S(1)}, f32[2,24,4,8,128]{4,3,2,1,0:T(8,128)}, u32[]{:S(2)}) copy-start(f32[2,24,4,8,128]{4,3,2,1,0:T(8,128)} %fusion.5) | copy-start | bytes 2359300
  101.4 6.1 %copy-start.6 = (bf16[2,192,512]{2,1,0:T(8,128)(2,1)S(1)}, bf16[2,192,512]{2,1,0:T(8,128)(2,1)}, u32[]{:S(2)}) copy-start(bf16[2,192,512]{2,1,0:T(8,128)(2,1)} %param.5) | copy-start | bytes 1179652
  103.6 3.1 %copy-start.15 = (bf16[1,2,4,128,128]{4,3,2,1,0:T(8,128)(2,1)}, bf16[1,2,4,128,128]{4,3,2,1,0:T(8,128)(2,1)S(1)}, u32[]{:S(2)}) copy-start(bf16[1,2,4,128,128]{4,3,2,1,0:T(8,128)(2,1)S(1)} %fusion.34) | copy-start | bytes 786436
  106.7 0.7 copy-start.2
  108.8 51.4 %all-gather.21.cloned.1.call-start = ((), (), s32[]{:S(2)}) async-start(), calls=%async_computation.7 | async-start | bytes 2621440 | tf_op jit(solution)/shard_map/all_gather | solution.py:21
  126.3 126.2 %reduce-scatter.4.cloned.1.call-start = ((), (), s32[]{:S(2)}) async-start(), calls=%async_computation.8 | async-start | bytes 4325376
  145.9 80.8 %all-to-all-start = ((bf16[8,2,192,512]{3,2,1,0:T(8,128)(2,1)}), bf16[8,2,192,512]{3,2,1,0:T(8,128)(2,1)S(1)}, u32[]{:S(2)}, u32[]{:S(2)}) async-start(bf16[8,2,192,512]{3,2,1,0:T(8,128)(2,1)} %bitcast.228), calls=%async_computation | async-start | bytes 6291456 | tf_op jit(solution)/shard_map/all_to_all | solution.py:38
  152.4 136.3 %all-gather.13.cloned.1.call-start = ((), (), s32[]{:S(2)}) async-start(), calls=%async_computation.3 | async-start | bytes 2621440 | tf_op jit(solution)/shard_map/all_gather | solution.py:21
  164.1 3.0 %copy-start.12 = (bf16[2,4,192,192]{3,2,1,0:T(8,128)(2,1)}, bf16[2,4,192,192]{3,2,1,0:T(8,128)(2,1)S(1)}, u32[]{:S(2)}) copy-start(bf16[2,4,192,192]{3,2,1,0:T(8,128)(2,1)S(1)} %select_convert_fusion) | copy-start | bytes 1769476
  228.0 64.0 %copy-start.9 = (bf16[2,192,512]{2,1,0:T(8,128)(2,1)S(1)}, bf16[2,192,512]{2,1,0:T(8,128)(2,1)}, u32[]{:S(2)}) copy-start(bf16[2,192,512]{2,1,0:T(8,128)(2,1)} %param.6) | copy-start | bytes 1179652
  228.0 64.3 %copy-start.7 = (bf16[2,192,512]{2,1,0:T(8,128)(2,1)S(1)}, bf16[2,192,512]{2,1,0:T(8,128)(2,1)}, u32[]{:S(2)}) copy-start(bf16[2,192,512]{2,1,0:T(8,128)(2,1)} %param.5) | copy-start | bytes 1179652
  228.0 64.3 %copy-start.13 = (bf16[2,4,192,192]{3,2,1,0:T(8,128)(2,1)S(1)}, bf16[2,4,192,192]{3,2,1,0:T(8,128)(2,1)}, u32[]{:S(2)}) copy-start(bf16[2,4,192,192]{3,2,1,0:T(8,128)(2,1)} %copy-done.12) | copy-start | bytes 1769476
  228.0 64.8 %copy-start.3 = (bf16[2,4,192,128]{3,2,1,0:T(8,128)(2,1)S(1)}, bf16[2,4,192,128]{3,2,1,0:T(8,128)(2,1)}, u32[]{:S(2)}) copy-start(bf16[2,4,192,128]{3,2,1,0:T(8,128)(2,1)} %copy-done.2) | copy-start | bytes 1179652
  228.0 64.8 %copy-start.11 = (bf16[2,4,192,192]{3,2,1,0:T(8,128)(2,1)S(1)}, bf16[2,4,192,192]{3,2,1,0:T(8,128)(2,1)}, u32[]{:S(2)}) copy-start(bf16[2,4,192,192]{3,2,1,0:T(8,128)(2,1)} %select_convert_fusion.1) | copy-start | bytes 1769476
Sparse Core Ops, SparseCore 0:
  10.4 18.8 all-gather.14
  31.6 33.7 all-gather.18
  68.0 33.3 all-gather.10
  108.9 15.3 all-gather.16
  126.5 33.7 all-gather.20
  164.0 88.4 reduce-scatter.3
  254.4 34.2 all-gather.12
